TPU v7x, 512 devices: a whole 4x8x8 slice. The times are simulated.
512 devices in a mesh: pipe: 16 (over y, x_lo), dp: 32 (over z, x_hi, core).
Axes of the slice: x: 4 (x_hi: 2, x_lo: 2; x = x_hi * 2 + x_lo), y: 8, z: 8, core: 2. Of those that a mesh axis runs over, the one named last changes fastest.
Arguments:
- hidden: float32 [256, 2048], P('dp', 'pipe'), may hold values from -6 to 6
- weight: float32 [131072, 2048], P(('pipe', 'dp')), may hold values from -0.375 to 0.375
- log_norm: float32 [256], replicated, may hold values from 14 to 17
- targets: int32 [256], replicated, may hold values from 0 to 131071
- loss_grad: float32 [256], replicated, may hold values from 0.5 to 2
Outputs:
- grad_hidden: float32 [256, 2048], P('dp', 'pipe')
- grad_weight: float32 [131072, 2048], P(('pipe', 'dp'))
All inputs are finite; a program needn't handle non-finite values.
Results may differ from a plain program's by a relative error of at most 0.0003.
Values sent between devices are 32-bit elements; how exact they have to be, the bound alone decides.
No kernel may reach another device: no remote copies, remote signals or barrier semaphores. Data moves between devices by JAX's collectives and lax.ppermute only.
A program may use at most 64 MiB of HBM per device.

v0:
```python
import jax
import jax.numpy as jnp
from jax import lax
from jax.sharding import PartitionSpec as P


def on_device(hidden, weight, log_norm, targets, loss_grad):
    vocab_rows = weight.shape[0]
    full_rows = lax.all_gather(hidden, "pipe", axis=1, tiled=True)
    all_tokens = lax.all_gather(full_rows, "dp", axis=0, tiled=True)
    shard_index = lax.axis_index("pipe") * lax.axis_size("dp") + lax.axis_index("dp")
    first_row = shard_index * vocab_rows
    logits = lax.dot_general(
        all_tokens,
        weight,
        (((1,), (1,)), ((), ())),
        precision=lax.Precision.HIGHEST,
        preferred_element_type=jnp.float32,
    )
    prob = jnp.exp(logits - log_norm[:, None])
    columns = first_row + jnp.arange(vocab_rows, dtype=jnp.int32)
    onehot = (targets[:, None] == columns[None, :]).astype(jnp.float32)
    dlogits = loss_grad[:, None] * (prob - onehot)
    grad_weight = lax.dot_general(
        dlogits,
        all_tokens,
        (((0,), (0,)), ((), ())),
        precision=lax.Precision.HIGHEST,
        preferred_element_type=jnp.float32,
    )
    token_part = lax.psum_scatter(
        jnp.dot(
            dlogits, weight, precision=lax.Precision.HIGHEST, preferred_element_type=jnp.float32
        ),
        "dp",
        scatter_dimension=0,
        tiled=True,
    )
    grad_hidden = lax.psum_scatter(token_part, "pipe", scatter_dimension=1, tiled=True)
    return (grad_hidden, grad_weight)


def solution(mesh):
    in_specs = (P("dp", "pipe"), P(("pipe", "dp"), None), P(), P(), P())
    out_specs = (P("dp", "pipe"), P(("pipe", "dp"), None))
    return jax.shard_map(
        on_device, mesh=mesh, in_specs=in_specs, out_specs=out_specs, check_vma=False
    )
```

profile of v0, /device:TPU:4, one launch (start us, length us, event | category | flops | bytes accessed | tf_op | source)
XLA Modules:
  0.0 343.6 jit_solution(5011547918847655677)
XLA Ops:
  7.2 0.0 copy-start
  7.2 0.0 all-gather.2.cloned.1.call-start
  7.2 36.6 %all_gather.6 = f32[8,2048]{1,0:T(8,128)} all-gather(f32[8,128]{1,0:T(8,128)} %param.5), channel_id=1, replica_groups=mesh['pipe'=16,'dp'=32] {'pipe'}, dimensions={1}, use_global_device_ids=true | all-gather | bytes 69632 | tf_op jit(solution)/shard_map/all_gather | solution.py:9
  43.9 0.0 all-gather.2.cloned.1.call-update
  43.9 0.0 reduce-scatter.3.cloned.1.call-start
  44.0 85.2 %all-gather.2.cloned.1.call-done = f32[256,2048]{1,0:T(8,128)} async-done(((f32[8,2048]{1,0:T(8,128)}), f32[256,2048]{1,0:T(8,128)}) %all-gather.2.cloned.1.call-update) | async-done | bytes 2097168 | tf_op jit(solution)/shard_map/all_gather | solution.py:10
  129.1 0.0 copy-done
  129.1 3.5 %fusion.2 = f32[256,256]{1,0:T(8,128)S(1)} fusion(f32[256,2048]{1,0:T(8,128)} %all-gather.2.cloned.1.call-done, f32[256,2048]{1,0:T(8,128)S(1)} %copy-done, s32[256]{0:T(256)S(1)} %iota_add_fusion, f32[256]{0:T(256)} %param.7, f32[256]{0:T(256)} %param.9, s32[256]{0:T(256)} %param.8), kind=kOutput, calls=%fused_computation.3 | convolution fusion | flops 1610940416 | bytes 4460544 | tf_op jit(solution)/shard_map/dot_general | solution.py:13
  132.6 3.2 fusion.3
  135.9 0.0 reduce-scatter.3.cloned.1.call-update
  135.9 0.0 reduce-scatter.5.cloned.1.call-start
  135.9 126.6 %reduce-scatter.3.cloned.1.call-done = f32[8,2048]{1,0:T(8,128)} async-done(((f32[256,2048]{1,0:T(8,128)}), f32[8,2048]{1,0:T(8,128)}) %reduce-scatter.3.cloned.1.call-update) | async-done | bytes 65552 | tf_op jit(solution)/shard_map/reduce_scatter | solution.py:31
  262.5 0.0 reduce-scatter.5.cloned.1.call-update
  262.5 4.8 %fusion.4 = f32[256,2048]{1,0:T(8,128)} fusion(f32[256,256]{1,0:T(8,128)S(1)} %fusion.2, f32[256,2048]{1,0:T(8,128)} %all-gather.2.cloned.1.call-done), kind=kOutput, calls=%fused_computation.6 | convolution fusion | flops 1610612736 | bytes 4456448 | tf_op jit(solution)/shard_map/dot_general | solution.py:24
  267.3 69.7 %reduce-scatter.5.cloned.1.call-done = f32[8,128]{1,0:T(8,128)} async-done(((f32[8,2048]{1,0:T(8,128)}), f32[8,128]{1,0:T(8,128)}) %reduce-scatter.5.cloned.1.call-update) | async-done | bytes 4112 | tf_op jit(solution)/shard_map/reduce_scatter | solution.py:39
  (1 shorter events, 0.0 us)
Async XLA Ops:
  7.2 122.0 %copy-start = (f32[256,2048]{1,0:T(8,128)S(1)}, f32[256,2048]{1,0:T(8,128)}, u32[]{:S(2)}) copy-start(f32[256,2048]{1,0:T(8,128)} %param.6) | copy-start | bytes 6291460
  7.2 121.9 %all-gather.2.cloned.1.call-start = ((), (), s32[]{:S(2)}) async-start(), calls=%async_computation.2 | async-start | bytes 2162688 | tf_op jit(solution)/shard_map/all_gather | solution.py:10
  43.9 218.6 %reduce-scatter.3.cloned.1.call-start = ((), (), s32[]{:S(2)}) async-start(), calls=%async_computation.3 | async-start | bytes 2162688 | tf_op jit(solution)/shard_map/reduce_scatter | solution.py:31
  135.9 201.1 %reduce-scatter.5.cloned.1.call-start = ((), (), s32[]{:S(2)}) async-start(), calls=%async_computation.4 | async-start | bytes 69632 | tf_op jit(solution)/shard_map/reduce_scatter | solution.py:39
Sparse Core Ops, SparseCore 0:
  44.0 85.0 all-gather.1
  136.0 126.4 reduce-scatter.2
  265.9 71.1 reduce-scatter.4
where the time goes:
time: 344 us
  waiting for transfers between devices  281 us (82%)
  blocking collectives  36.6 us (11%)
  between operations  13.8 us (4%)
  matrix products  11.5 us (3%)
    reduce_scatter x1, waiting for transfers between devices, on_device(): lax.psum_scatter(jnp.dot(dlogits, weight, precision=lax.Precision.HIGHEST...  127 us
    all_gather x1, waiting for transfers between devices, on_device(): all_tokens = lax.all_gather(full_rows, 'dp', axis=0, tiled=True)  85.2 us
    reduce_scatter x1, waiting for transfers between devices, on_device(): lax.psum_scatter(token_part, 'pipe', scatter_dimension=1, tiled=True)  69.7 us
    all_gather x1, blocking collectives, on_device(): full_rows = lax.all_gather(hidden, 'pipe', axis=1, tiled=True)  36.6 us
  transfers between devices with their start and end apart: 3, of which 3 were waited for; matrix products, arithmetic and copies ran while one was open for 1% of the time, Pallas kernels for 0%

commit v1 on v0

v1 whole, which is shorter than its diff:
```python
import jax
import jax.numpy as jnp
from jax import lax
from jax.experimental import pallas as pl
from jax.experimental.pallas import tpu as pltpu
from jax.sharding import Mesh
from jax.sharding import PartitionSpec as P

PIPE = ("yh", "yl", "xl")
DP = ("zh", "zl", "xh", "c")
SIZES = (4, 2, 2, 4, 2, 2, 2)
FAR = ("yh", "zh")
NEAR = ("yl", "xl", "zl", "xh")

TOK = 128
ROWS = 256
D = 2048
CHUNK = 512
NCH = D // CHUNK
TILES = (4, 4, 4, 4, 8, 128)


def swap(x):
    return lax.ppermute(x, "c", [(0, 1), (1, 0)])


def spread(block, axes):
    n = lax.axis_size(axes)
    return lax.all_to_all(
        jnp.broadcast_to(block[None], (n, *block.shape)), axes, 0, 0, tiled=True
    )


def parts(a):
    high = a.astype(jnp.bfloat16)
    return high, (a - high.astype(jnp.float32)).astype(jnp.bfloat16)


def dot(a, b, dims):
    return lax.dot_general(a, b, (dims, ((), ())), preferred_element_type=jnp.float32)


def dot3(a, b_high, b_low, dims):
    high, both = a
    m = high.shape[0]
    t = dot(both, b_high, dims)
    return t[:m] + t[m:] + dot(high, b_low, dims)


def columns_of(x_ref, j):
    return jnp.concatenate([x_ref[f, :, j].reshape(TOK, 128) for f in range(4)], axis=1)


def stacked(a):
    high, low = parts(a)
    return high, jnp.concatenate([high, low], axis=0)


def head_kernel(
    first_ref, vec_ref, x_ref, w0, w1, dl_ref, part_ref, wbuf, high, low, sems
):
    copies = {}
    for j in range(NCH):
        cols = pl.ds(j * CHUNK, CHUNK)
        for k, w in ((0, w0), (1, w1)):
            copies[k, j] = pltpu.make_async_copy(
                w.at[:, cols], wbuf.at[k, :, cols], sems.at[k, j]
            )
            copies[k, j].start()
    acc = [jnp.zeros((TOK, ROWS), jnp.float32) for _ in range(2)]
    for j in range(NCH):
        cols = pl.ds(j * CHUNK, CHUNK)
        x = stacked(columns_of(x_ref, j))
        for k in range(2):
            copies[k, j].wait()
            h, l = parts(wbuf[k, :, cols])
            high[k, :, cols] = h
            low[k, :, cols] = l
            acc[k] = acc[k] + dot3(x, h, l, ((1,), (1,)))
    log_norm, grad, target = vec_ref[:, 0:1], vec_ref[:, 1:2], vec_ref[:, 2:3]
    target = target.astype(jnp.int32)
    d = []
    for k in range(2):
        prob = jnp.exp(acc[k] - log_norm)
        column = first_ref[k] + lax.broadcasted_iota(jnp.int32, (TOK, ROWS), 1)
        dl = grad * (prob - (target == column).astype(jnp.float32))
        dl_ref[k] = dl
        d.append(stacked(dl))
    for j in range(NCH):
        cols = pl.ds(j * CHUNK, CHUNK)
        part = dot3(d[0], high[0, :, cols], low[0, :, cols], ((1,), (0,)))
        part += dot3(d[1], high[1, :, cols], low[1, :, cols], ((1,), (0,)))
        for f in range(4):
            part_ref[f, :, j] = part[:, f * 128 : (f + 1) * 128].reshape(4, 4, 8, 128)


def head(first, vec, x, w0, w1):
    vmem = pl.BlockSpec(memory_space=pltpu.VMEM)
    return pl.pallas_call(
        head_kernel,
        out_shape=(
            jax.ShapeDtypeStruct((2, TOK, ROWS), jnp.float32),
            jax.ShapeDtypeStruct(TILES, jnp.float32),
        ),
        in_specs=[
            pl.BlockSpec(memory_space=pltpu.SMEM),
            vmem,
            vmem,
            pl.BlockSpec(memory_space=pltpu.HBM),
            pl.BlockSpec(memory_space=pltpu.HBM),
        ],
        out_specs=(vmem, vmem),
        scratch_shapes=[
            pltpu.VMEM((2, ROWS, D), jnp.float32),
            pltpu.VMEM((2, ROWS, D), jnp.bfloat16),
            pltpu.VMEM((2, ROWS, D), jnp.bfloat16),
            pltpu.SemaphoreType.DMA((2, NCH)),
        ],
        compiler_params=pltpu.CompilerParams(vmem_limit_bytes=24 << 20),
        cost_estimate=pl.CostEstimate(
            flops=12 * TOK * ROWS * D * 2,
            bytes_accessed=6 << 20,
            transcendentals=2 * TOK * ROWS,
        ),
        name="head",
    )(first, vec, x, w0, w1)


def weight_grad_kernel(d0_ref, d1_ref, x0_ref, x1_ref, out_ref):
    d = jnp.concatenate([d0_ref[...].T, d1_ref[...].T], axis=1)
    d = stacked(d)
    for j in range(NCH):
        x = jnp.concatenate([columns_of(x0_ref, j), columns_of(x1_ref, j)], axis=0)
        out_ref[:, pl.ds(j * CHUNK, CHUNK)] = dot3(d, *parts(x), ((1,), (0,)))


def weight_grad(d0, d1, x0, x1):
    vmem = pl.BlockSpec(memory_space=pltpu.VMEM)
    return pl.pallas_call(
        weight_grad_kernel,
        out_shape=jax.ShapeDtypeStruct((ROWS, D), jnp.float32),
        in_specs=[vmem] * 4,
        out_specs=vmem,
        compiler_params=pltpu.CompilerParams(vmem_limit_bytes=24 << 20),
        cost_estimate=pl.CostEstimate(
            flops=6 * 2 * TOK * ROWS * D, bytes_accessed=5 << 20, transcendentals=0
        ),
        name="weight_grad",
    )(d0, d1, x0, x1)


def sum_kernel(x_ref, out_ref):
    total = x_ref[0]
    for i in range(1, x_ref.shape[0]):
        total = total + x_ref[i]
    out_ref[...] = total


def local_sum(x):
    vmem = pl.BlockSpec(memory_space=pltpu.VMEM)
    return pl.pallas_call(
        sum_kernel,
        out_shape=jax.ShapeDtypeStruct(x.shape[1:], jnp.float32),
        in_specs=[vmem],
        out_specs=vmem,
        compiler_params=pltpu.CompilerParams(vmem_limit_bytes=8 << 20),
        name="local_sum",
    )(x)


def on_device(hidden, weight, log_norm, targets, loss_grad):
    c = lax.axis_index("c")
    shard = lax.axis_index(PIPE + DP)
    far = spread(hidden, FAR)
    own_weight, far = lax.optimization_barrier((weight, far))
    other_weight = swap(own_weight)
    near = spread(far, NEAR).reshape(TILES)

    vec = jnp.stack([log_norm, loss_grad, targets.astype(jnp.float32)], axis=1)
    vec = vec.reshape(4, 2, 2, 2, 8, 3)
    vec = lax.dynamic_index_in_dim(vec, c, axis=3, keepdims=False)
    vec = vec.transpose(1, 2, 0, 3, 4).reshape(TOK, 3)
    first = jnp.stack([shard, shard + 1 - 2 * c]).astype(jnp.int32) * ROWS

    dl, part = head(first, vec, near, weight, other_weight)

    got = lax.all_to_all(part.reshape(16, 16, 8, 128), NEAR, 0, 0, tiled=True)
    got = lax.all_to_all(local_sum(got), FAR, 0, 0, tiled=True)
    got = local_sum(got)

    near, dl = lax.optimization_barrier((near, dl))
    grad_weight = weight_grad(dl[0], swap(dl[1]), near, swap(near))
    return (got, grad_weight)


def solution(mesh):
    fine = Mesh(mesh.devices.reshape(SIZES), PIPE + DP)
    in_specs = (P(DP, PIPE), P(PIPE + DP, None), P(), P(), P())
    out_specs = (P(DP, PIPE), P(PIPE + DP, None))
    return jax.shard_map(
        on_device, mesh=fine, in_specs=in_specs, out_specs=out_specs, check_vma=False
    )
```

time: 344 us -> 101 us (0.29)
  the two profiles are of different devices: /device:TPU:4 before, /device:TPU:10 now
where the time goes in v1:
time: 101 us
  waiting for transfers between devices  38.3 us (38%)
  blocking collectives  27 us (27%)
  starting transfers between devices  21.9 us (22%)
  Pallas kernels  9.64 us (10%)
  local copies, waits for them, and re-layouts  3.05 us (3%)
    all_to_all x1, blocking collectives, spread(): lax.all_to_all(jnp.broadcast_to(block[None], (n, *block.shape)), axes, 0,...  27 us
    all_to_all x1, waiting for transfers between devices, spread(): lax.all_to_all(jnp.broadcast_to(block[None], (n, *block.shape)), axes, 0,...  17.2 us
    all_to_all x1, waiting for transfers between devices, on_device(): got = lax.all_to_all(part.reshape(16, 16, 8, 128), NEAR, 0, 0, tiled=True)  11.1 us
    all_to_all x1, waiting for transfers between devices, on_device(): got = lax.all_to_all(local_sum(got), FAR, 0, 0, tiled=True)  9.99 us
    all_to_all x1, starting transfers between devices, spread(): lax.all_to_all(jnp.broadcast_to(block[None], (n, *block.shape)), axes, 0,...  6.69 us
    ppermute x3, starting transfers between devices, swap(): return lax.ppermute(x, 'c', [(0, 1), (1, 0)])  6.21 us
    pallas_call x1, Pallas kernels, head(): pl.pallas_call(head_kernel, out_shape=(jax.ShapeDtypeStruct((2, TOK, ROWS...  5.99 us
    all_to_all x1, starting transfers between devices, on_device(): got = lax.all_to_all(part.reshape(16, 16, 8, 128), NEAR, 0, 0, tiled=True)  5.53 us
  transfers between devices with their start and end apart: 6, of which 3 were waited for; matrix products, arithmetic and copies ran while one was open for 2% of the time, Pallas kernels for 3%

profile of v1, /device:TPU:10, one launch (start us, length us, event | category | flops | bytes accessed | tf_op | source)
XLA Modules:
  0.0 100.8 jit_solution(3051332333786042885)
XLA Ops:
  0.6 0.0 copy-start
  0.7 0.8 broadcast_in_dim.4
  1.5 27.0 %all_to_all.20 = f32[16,8,128]{2,1,0:T(8,128)S(1)} all-to-all(f32[16,8,128]{2,1,0:T(8,128)S(1)} %broadcast_in_dim.4), channel_id=1, replica_groups=mesh['yh'=4,'yl'=2,'xl'=2,'zh'=4,'zl'=2,'xh'=2,'c'=2] {'yh','zh'}, dimensions={0} | all-to-all | bytes 131072 | tf_op jit(solution)/shard_map/all_to_all | solution.py:29
  28.5 1.9 %collective-permute-start = (f32[256,2048]{1,0:T(8,128)}, f32[256,2048]{1,0:T(8,128)}, u32[]{:S(2)}, u32[]{:S(2)}) collective-permute-start(f32[256,2048]{1,0:T(8,128)} %w0.1), channel_id=1, source_target_pairs={{0,1},{1,0},{2,3},{3,2},{4,5},{5,4},{6,7},{7,6},{8,9},{9,8},{10,11... | collective-permute-start | bytes 6291464 | tf_op jit(solution)/shard_map/ppermute | solution.py:24
  30.4 1.1 %broadcast_in_dim.5 = f32[16,16,8,128]{3,2,1,0:T(8,128)} broadcast(f32[16,8,128]{2,1,0:T(8,128)S(1)} %all_to_all.20), dimensions={1,2,3} | broadcast | bytes 1114112 | tf_op jit(solution)/shard_map/broadcast_in_dim | solution.py:30
  31.5 6.7 %all-to-all-start.1 = ((f32[16,16,8,128]{3,2,1,0:T(8,128)}), f32[16,16,8,128]{3,2,1,0:T(8,128)S(1)}, u32[]{:S(2)}, u32[]{:S(2)}) async-start(f32[16,16,8,128]{3,2,1,0:T(8,128)} %broadcast_in_dim.5), calls=%async_computation.1 | async-start | bytes 2097152 | tf_op jit(solution)/shard_map/all_to_all | solution.py:29
  38.2 0.1 stack.26
  38.3 0.1 stack.24
  38.4 0.1 stack.25
  38.6 0.2 copy.8
  38.8 0.1 add_multiply_fusion.first_ref
  38.8 17.2 %all-to-all-done.1 = f32[16,16,8,128]{3,2,1,0:T(8,128)S(1)} async-done(((f32[16,16,8,128]{3,2,1,0:T(8,128)}), f32[16,16,8,128]{3,2,1,0:T(8,128)S(1)}, u32[]{:S(2)}, u32[]{:S(2)}) %all-to-all-start.1) | async-done | bytes 1048608 | tf_op jit(solution)/shard_map/all_to_all | solution.py:29
  56.1 0.0 collective-permute-done.w1
  56.1 6.0 %head.1 = (f32[2,128,256]{2,1,0:T(8,128)S(1)}, f32[4,4,4,4,8,128]{5,4,3,2,1,0:T(8,128)}) custom-call(s32[2]{0:T(128)S(1)} %add_multiply_fusion.first_ref, f32[128,3]{1,0:T(8,128)S(1)} %bitcast.17, f32[4,4,4,4,8,128]{5,4,3,2,1,0:T(8,128)S(1)} %bitcast.14, f32[256,2048]{1,0:T(8,128)S(1)} %copy-done, f32[256,2048]{1,0:T(8,128)} %collective-permute-done.w1), custom_call_target="tpu_custom_call" | custom-call | flops 1610612736 | bytes 6291456 | tf_op jit(solution)/shard_map/head/pallas_call | solution.py:99
  62.1 5.5 %all-to-all-start.2 = ((f32[16,16,8,128]{3,2,1,0:T(8,128)}), f32[16,16,8,128]{3,2,1,0:T(8,128)S(1)}, u32[]{:S(2)}, u32[]{:S(2)}) async-start(f32[16,16,8,128]{3,2,1,0:T(8,128)} %bitcast.6), calls=%async_computation.2 | async-start | bytes 2097152 | tf_op jit(solution)/shard_map/all_to_all | solution.py:187
  67.6 1.9 %collective-permute-start.2 = (f32[4,4,4,4,8,128]{5,4,3,2,1,0:T(8,128)S(1)}, f32[4,4,4,4,8,128]{5,4,3,2,1,0:T(8,128)S(1)}, u32[]{:S(2)}, u32[]{:S(2)}) collective-permute-start(f32[4,4,4,4,8,128]{5,4,3,2,1,0:T(8,128)S(1)} %bitcast.15), channel_id=1, source_target_pairs={{0,1},{1,0},{2,3},{3,2},{4,5},{5,4},{6,7},{7,6},{8,9},{9,8},{10,11... | collective-permute-start | bytes 3145736 | tf_op jit(solution)/shard_map/ppermute | solution.py:24
  69.5 0.7 slice_bitcast_fusion
  70.2 2.4 %collective-permute-start.1 = (f32[128,256]{1,0:T(8,128)}, f32[128,256]{1,0:T(8,128)S(1)}, u32[]{:S(2)}, u32[]{:S(2)}) collective-permute-start(f32[128,256]{1,0:T(8,128)} %get-tuple-element.14), channel_id=1, source_target_pairs={{0,1},{1,0},{2,3},{3,2},{4,5},{5,4},{6,7},{7,6},{8,9},{9,8},{10,11... | collective-permute-start | bytes 393224 | tf_op jit(solution)/shard_map/ppermute | solution.py:24
  72.6 11.1 %all-to-all-done.2.x_ref = f32[16,16,8,128]{3,2,1,0:T(8,128)S(1)} async-done(((f32[16,16,8,128]{3,2,1,0:T(8,128)}), f32[16,16,8,128]{3,2,1,0:T(8,128)S(1)}, u32[]{:S(2)}, u32[]{:S(2)}) %all-to-all-start.2) | async-done | bytes 1048608 | tf_op jit(solution)/shard_map/all_to_all | solution.py:187
  83.7 0.7 local_sum.2
  84.3 3.5 %all-to-all-start.3 = ((f32[16,8,128]{2,1,0:T(8,128)}), f32[16,8,128]{2,1,0:T(8,128)S(1)}, u32[]{:S(2)}, u32[]{:S(2)}) async-start(f32[16,8,128]{2,1,0:T(8,128)} %local_sum.2), calls=%async_computation.3 | async-start | bytes 131072 | tf_op jit(solution)/shard_map/all_to_all | solution.py:188
  87.9 2.4 %weight_grad.1 = f32[256,2048]{1,0:T(8,128)} custom-call(f32[128,256]{1,0:T(8,128)S(1)} %get-tuple-element.15.d0_ref, f32[128,256]{1,0:T(8,128)S(1)} %collective-permute-done.1.d1_ref, f32[4,4,4,4,8,128]{5,4,3,2,1,0:T(8,128)S(1)} %bitcast.16, f32[4,4,4,4,8,128]{5,4,3,2,1,0:T(8,128)S(1)} %collective-permute-done.2.x1_ref), custom_call_target="tpu_custom_call" | custom-call | flops 805306368 | bytes 5242880 | tf_op jit(solution)/shard_map/weight_grad/pallas_call | solution.py:139
  90.2 10.0 %all-to-all-done.3.x_ref = f32[16,8,128]{2,1,0:T(8,128)S(1)} async-done(((f32[16,8,128]{2,1,0:T(8,128)}), f32[16,8,128]{2,1,0:T(8,128)S(1)}, u32[]{:S(2)}, u32[]{:S(2)}) %all-to-all-start.3) | async-done | bytes 65568 | tf_op jit(solution)/shard_map/all_to_all | solution.py:188
  100.2 0.6 local_sum.3
  (12 shorter events, 0.1 us)
Async XLA Ops:
  0.6 55.4 %copy-start = (f32[256,2048]{1,0:T(8,128)S(1)}, f32[256,2048]{1,0:T(8,128)}, u32[]{:S(2)}) copy-start(f32[256,2048]{1,0:T(8,128)} %w0.1) | copy-start | bytes 6291460
  0.6 37.6 %copy-start.3 = (s32[256]{0:T(256)S(1)}, s32[256]{0:T(256)}, u32[]{:S(2)}) copy-start(s32[256]{0:T(256)} %param.8) | copy-start | bytes 3076
  0.7 37.7 %copy-start.1 = (f32[256]{0:T(256)S(1)}, f32[256]{0:T(256)}, u32[]{:S(2)}) copy-start(f32[256]{0:T(256)} %param.7) | copy-start | bytes 3076
  0.7 37.8 %copy-start.2 = (f32[256]{0:T(256)S(1)}, f32[256]{0:T(256)}, u32[]{:S(2)}) copy-start(f32[256]{0:T(256)} %param.9) | copy-start | bytes 3076
  28.5 27.6 %collective-permute-start = (f32[256,2048]{1,0:T(8,128)}, f32[256,2048]{1,0:T(8,128)}, u32[]{:S(2)}, u32[]{:S(2)}) collective-permute-start(f32[256,2048]{1,0:T(8,128)} %w0.1), channel_id=1, source_target_pairs={{0,1},{1,0},{2,3},{3,2},{4,5},{5,4},{6,7},{7,6},{8,9},{9,8},{10,11... | collective-permute-start | bytes 6291464 | tf_op jit(solution)/shard_map/ppermute | solution.py:24
  31.5 24.6 %all-to-all-start.1 = ((f32[16,16,8,128]{3,2,1,0:T(8,128)}), f32[16,16,8,128]{3,2,1,0:T(8,128)S(1)}, u32[]{:S(2)}, u32[]{:S(2)}) async-start(f32[16,16,8,128]{3,2,1,0:T(8,128)} %broadcast_in_dim.5), calls=%async_computation.1 | async-start | bytes 2097152 | tf_op jit(solution)/shard_map/all_to_all | solution.py:29
  62.1 21.6 %all-to-all-start.2 = ((f32[16,16,8,128]{3,2,1,0:T(8,128)}), f32[16,16,8,128]{3,2,1,0:T(8,128)S(1)}, u32[]{:S(2)}, u32[]{:S(2)}) async-start(f32[16,16,8,128]{3,2,1,0:T(8,128)} %bitcast.6), calls=%async_computation.2 | async-start | bytes 2097152 | tf_op jit(solution)/shard_map/all_to_all | solution.py:187
  67.6 20.3 %collective-permute-start.2 = (f32[4,4,4,4,8,128]{5,4,3,2,1,0:T(8,128)S(1)}, f32[4,4,4,4,8,128]{5,4,3,2,1,0:T(8,128)S(1)}, u32[]{:S(2)}, u32[]{:S(2)}) collective-permute-start(f32[4,4,4,4,8,128]{5,4,3,2,1,0:T(8,128)S(1)} %bitcast.15), channel_id=1, source_target_pairs={{0,1},{1,0},{2,3},{3,2},{4,5},{5,4},{6,7},{7,6},{8,9},{9,8},{10,11... | collective-permute-start | bytes 3145736 | tf_op jit(solution)/shard_map/ppermute | solution.py:24
  70.2 17.7 %collective-permute-start.1 = (f32[128,256]{1,0:T(8,128)}, f32[128,256]{1,0:T(8,128)S(1)}, u32[]{:S(2)}, u32[]{:S(2)}) collective-permute-start(f32[128,256]{1,0:T(8,128)} %get-tuple-element.14), channel_id=1, source_target_pairs={{0,1},{1,0},{2,3},{3,2},{4,5},{5,4},{6,7},{7,6},{8,9},{9,8},{10,11... | collective-permute-start | bytes 393224 | tf_op jit(solution)/shard_map/ppermute | solution.py:24
  84.3 15.9 %all-to-all-start.3 = ((f32[16,8,128]{2,1,0:T(8,128)}), f32[16,8,128]{2,1,0:T(8,128)S(1)}, u32[]{:S(2)}, u32[]{:S(2)}) async-start(f32[16,8,128]{2,1,0:T(8,128)} %local_sum.2), calls=%async_computation.3 | async-start | bytes 131072 | tf_op jit(solution)/shard_map/all_to_all | solution.py:188

commit v2 on v1

v2 whole, which is shorter than its diff:
```python
import jax
import jax.numpy as jnp
from jax import lax
from jax.experimental import pallas as pl
from jax.experimental.pallas import tpu as pltpu
from jax.sharding import Mesh
from jax.sharding import PartitionSpec as P

PIPE = ("yh", "yl", "xl")
DP = ("zh", "zl", "xh", "c")
SIZES = (4, 2, 2, 4, 2, 2, 2)


def device(y, x, z, c):
    return y * 64 + x % 2 * 32 + z * 4 + x // 2 * 2 + c


def pairs(n, c):
    return [((i + 2 * c) % n, i + 1) for i in range(0, n, 2)]


FAR = [
    [
        device(2 * yh + yl, 2 * xh + xl, 2 * zh + zl, c)
        for yh in range(4)
        for zh in range(4)
        for xh in range(2)
    ]
    for c in range(2)
    for yl in range(2)
    for xl in range(2)
    for zl in range(2)
]
NEAR = [
    [device(y, x, z, c) for y in ys for x in xs for z in zs]
    for c in range(2)
    for ys in pairs(8, c)
    for xs in pairs(4, c)
    for zs in pairs(8, c)
]

TOK = 128
ROWS = 256
D = 2048
CHUNK = 512
SPLIT_VMEM, HEAD_VMEM = 62, 50
PIECES = 4
NCH = D // CHUNK
TILES = (4, 2, 4, 8, 8, 128)


def swap(x):
    return lax.ppermute(x, "c", [(0, 1), (1, 0)])


def exchange(x, groups):
    return lax.all_to_all(
        x, PIPE + DP, 0, 0, axis_index_groups=groups, tiled=True
    )


def spread(block, groups):
    n = len(groups[0])
    return exchange(jnp.broadcast_to(block[None], (n, *block.shape)), groups)


def parts(a):
    high = a.astype(jnp.bfloat16)
    return high, (a - high.astype(jnp.float32)).astype(jnp.bfloat16)


def dot(a, b, dims):
    return lax.dot_general(a, b, (dims, ((), ())), preferred_element_type=jnp.float32)


def dot3(a, b_high, b_low, dims):
    high, both = a
    m = high.shape[0]
    t = dot(both, b_high, dims)
    return t[:m] + t[m:] + dot(high, b_low, dims)


def columns_of(x_ref, j):
    return jnp.concatenate([x_ref[f, :, j].reshape(TOK, 128) for f in range(4)], axis=1)


def stacked(a):
    high, low = parts(a)
    return high, jnp.concatenate([high, low], axis=0)


def split_kernel(w0_ref, w1_ref, high_ref, low_ref):
    for k, w in ((0, w0_ref), (1, w1_ref)):
        rows = pl.ds(k * ROWS, ROWS)
        high_ref[rows], low_ref[rows] = parts(w[...])


def split(w0, w1):
    vmem = pl.BlockSpec(memory_space=pltpu.VMEM)
    out = jax.ShapeDtypeStruct((2 * ROWS, D), jnp.bfloat16)
    return pl.pallas_call(
        split_kernel,
        out_shape=(out, out),
        in_specs=[vmem, vmem],
        out_specs=(vmem, vmem),
        compiler_params=pltpu.CompilerParams(vmem_limit_bytes=SPLIT_VMEM << 20),
        cost_estimate=pl.CostEstimate(
            flops=6 * ROWS * D, bytes_accessed=8 << 20, transcendentals=0
        ),
        name="split",
    )(w0, w1)


def head_kernel(
    first_ref,
    vec_ref,
    x_ref,
    high_ref,
    low_ref,
    dl0_ref,
    dl1_ref,
    part_ref,
    high,
    low,
    xs,
    out,
    ins,
    outs,
):
    fetches = []
    for p, (src, dst) in enumerate(((high_ref, high), (low_ref, low))):
        for i in range(PIECES):
            rows = pl.ds(i * (2 * ROWS // PIECES), 2 * ROWS // PIECES)
            fetches.append(
                pltpu.make_async_copy(src.at[rows], dst.at[rows], ins.at[p, i])
            )
            fetches[-1].start()
    for j in range(NCH):
        for f in range(4):
            cols = pl.ds(j * CHUNK + f * 128, 128)
            xs[:TOK, cols], xs[TOK:, cols] = parts(x_ref[f, :, j].reshape(TOK, 128))
    for fetch in fetches[:PIECES]:
        fetch.wait()
    both = dot(xs[...], high[...], ((1,), (1,)))
    for fetch in fetches[PIECES:]:
        fetch.wait()
    logits = both[:TOK] + both[TOK:] + dot(xs[:TOK], low[...], ((1,), (1,)))
    log_norm, grad, target = vec_ref[:, 0:1], vec_ref[:, 1:2], vec_ref[:, 2:3]
    target = target.astype(jnp.int32)
    d = []
    for k, dl_ref in ((0, dl0_ref), (1, dl1_ref)):
        prob = jnp.exp(logits[:, k * ROWS : (k + 1) * ROWS] - log_norm)
        column = first_ref[k] + lax.broadcasted_iota(jnp.int32, (TOK, ROWS), 1)
        dl = grad * (prob - (target == column).astype(jnp.float32))
        dl_ref[...] = dl
        d.append(stacked(dl))
    copies = []
    for j in range(NCH):
        cols = pl.ds(j * CHUNK, CHUNK)
        part = dot3(d[0], high[:ROWS, cols], low[:ROWS, cols], ((1,), (0,)))
        part += dot3(d[1], high[ROWS:, cols], low[ROWS:, cols], ((1,), (0,)))
        for f in range(4):
            out[j, f] = part[:, f * 128 : (f + 1) * 128].reshape(2, 8, 8, 128)
            copies.append(
                pltpu.make_async_copy(out.at[j, f], part_ref.at[f, :, j], outs.at[j, f])
            )
            copies[-1].start()
    for copy in copies:
        copy.wait()


def head(first, vec, x, high, low):
    vmem = pl.BlockSpec(memory_space=pltpu.VMEM)
    hbm = pl.BlockSpec(memory_space=pl.ANY)
    dl = jax.ShapeDtypeStruct((TOK, ROWS), jnp.float32)
    return pl.pallas_call(
        head_kernel,
        out_shape=(dl, dl, jax.ShapeDtypeStruct(TILES, jnp.float32)),
        in_specs=[pl.BlockSpec(memory_space=pltpu.SMEM), vmem, vmem, hbm, hbm],
        out_specs=(vmem, vmem, hbm),
        scratch_shapes=[
            pltpu.VMEM((2 * ROWS, D), jnp.bfloat16),
            pltpu.VMEM((2 * ROWS, D), jnp.bfloat16),
            pltpu.VMEM((2 * TOK, D), jnp.bfloat16),
            pltpu.VMEM((NCH, 4, 2, 8, 8, 128), jnp.float32),
            pltpu.SemaphoreType.DMA((2, PIECES)),
            pltpu.SemaphoreType.DMA((NCH, 4)),
        ],
        compiler_params=pltpu.CompilerParams(vmem_limit_bytes=HEAD_VMEM << 20),
        cost_estimate=pl.CostEstimate(
            flops=12 * TOK * ROWS * D * 2,
            bytes_accessed=6 << 20,
            transcendentals=2 * TOK * ROWS,
        ),
        name="head",
    )(first, vec, x, high, low)


def weight_grad_kernel(d0_ref, d1_ref, x0_ref, x1_ref, out_ref):
    d = jnp.concatenate([d0_ref[...].T, d1_ref[...].T], axis=1)
    d = stacked(d)
    for j in range(NCH):
        x = jnp.concatenate([columns_of(x0_ref, j), columns_of(x1_ref, j)], axis=0)
        out_ref[:, pl.ds(j * CHUNK, CHUNK)] = dot3(d, *parts(x), ((1,), (0,)))


def weight_grad(d0, d1, x0, x1):
    vmem = pl.BlockSpec(memory_space=pltpu.VMEM)
    return pl.pallas_call(
        weight_grad_kernel,
        out_shape=jax.ShapeDtypeStruct((ROWS, D), jnp.float32),
        in_specs=[vmem] * 4,
        out_specs=vmem,
        compiler_params=pltpu.CompilerParams(vmem_limit_bytes=24 << 20),
        cost_estimate=pl.CostEstimate(
            flops=6 * 2 * TOK * ROWS * D, bytes_accessed=5 << 20, transcendentals=0
        ),
        name="weight_grad",
    )(d0, d1, x0, x1)


def sum_kernel(x_ref, out_ref):
    total = x_ref[0]
    for i in range(1, x_ref.shape[0]):
        total = total + x_ref[i]
    out_ref[...] = total


def local_sum(x):
    vmem = pl.BlockSpec(memory_space=pltpu.VMEM)
    return pl.pallas_call(
        sum_kernel,
        out_shape=jax.ShapeDtypeStruct(x.shape[1:], jnp.float32),
        in_specs=[vmem],
        out_specs=vmem,
        compiler_params=pltpu.CompilerParams(vmem_limit_bytes=8 << 20),
        name="local_sum",
    )(x)


def on_device(hidden, weight, log_norm, targets, loss_grad):
    c = lax.axis_index("c")
    shard = lax.axis_index(PIPE + DP)

    vec = jnp.stack([log_norm, loss_grad, targets.astype(jnp.float32)], axis=1)
    vec = vec.reshape(4, 2, 2, 2, 8, 3)
    vec = lax.dynamic_index_in_dim(vec, c, axis=3, keepdims=False)
    vec = vec.transpose(1, 0, 2, 3, 4).reshape(TOK, 3)
    first = jnp.stack([shard, shard + 1 - 2 * c]).astype(jnp.int32) * ROWS

    far = spread(hidden, FAR)
    other_weight = swap(weight)
    near = spread(far, NEAR).reshape(TILES)
    high, low = split(weight, other_weight)
    dl0, dl1, part = head(first, vec, near, high, low)
    got = part.reshape(8, 32, 8, 128)
    got = exchange(got, NEAR)
    got = local_sum(got)
    got = exchange(got, FAR)
    got = local_sum(got)
    other_near = swap(near)
    other_dl = swap(dl1)
    grad_weight = weight_grad(dl0, other_dl, near, other_near)
    return (got, grad_weight)


def solution(mesh):
    fine = Mesh(mesh.devices.reshape(SIZES), PIPE + DP)
    in_specs = (P(DP, PIPE), P(PIPE + DP, None), P(), P(), P())
    out_specs = (P(DP, PIPE), P(PIPE + DP, None))
    return jax.shard_map(
        on_device, mesh=fine, in_specs=in_specs, out_specs=out_specs, check_vma=False
    )
```

time: 101 us -> 96.9 us (0.959)
  the two profiles are of different devices: /device:TPU:10 before, /device:TPU:1 now
where the time goes in v2:
time: 96.9 us; the launch traced here: 96.4 us
  starting transfers between devices  26.9 us (28%)
  blocking collectives  26.3 us (27%)
  waiting for transfers between devices  25.1 us (26%)
  Pallas kernels  15 us (15%)
  local copies, waits for them, and re-layouts  2.2 us (2%)
    all_to_all x1, blocking collectives, exchange(): lax.all_to_all(x, PIPE + DP, 0, 0, axis_index_groups=groups, tiled=True)  26.3 us
    all_to_all x3, waiting for transfers between devices, exchange(): lax.all_to_all(x, PIPE + DP, 0, 0, axis_index_groups=groups, tiled=True)  23.8 us
    all_to_all x3, starting transfers between devices, exchange(): lax.all_to_all(x, PIPE + DP, 0, 0, axis_index_groups=groups, tiled=True)  14.2 us
    ppermute x3, starting transfers between devices, swap(): return lax.ppermute(x, 'c', [(0, 1), (1, 0)])  12.7 us
    pallas_call x1, Pallas kernels, head(): pl.pallas_call(head_kernel, out_shape=(dl, dl, jax.ShapeDtypeStruct(TILES...  5.41 us
    pallas_call x1, Pallas kernels, split(): pl.pallas_call(split_kernel, out_shape=(out, out), in_specs=[vmem, vmem],...  4.66 us
    pallas_call x1, Pallas kernels, weight_grad(): pl.pallas_call(weight_grad_kernel, out_shape=jax.ShapeDtypeStruct((ROWS,...  3.58 us
  transfers between devices with their start and end apart: 6, of which 4 were waited for; matrix products, arithmetic and copies ran while one was open for 2% of the time, Pallas kernels for 9%

profile of v2, /device:TPU:1, one launch (start us, length us, event | category | flops | bytes accessed | tf_op | source)
XLA Modules:
  0.0 96.4 jit_solution(13146449815096279883)
XLA Ops:
  0.7 8.9 %collective-permute-start = (f32[256,2048]{1,0:T(8,128)}, f32[256,2048]{1,0:T(8,128)}, u32[]{:S(2)}, u32[]{:S(2)}) collective-permute-start(f32[256,2048]{1,0:T(8,128)} %w0_ref.1), channel_id=1, source_target_pairs={{0,1},{1,0},{2,3},{3,2},{4,5},{5,4},{6,7},{7,6},{8,9},{9,8},{10,11... | collective-permute-start | bytes 6291464 | tf_op jit(solution)/shard_map/ppermute | solution.py:53
  9.5 0.7 broadcast_in_dim.4
  10.2 26.3 %all_to_all.20 = f32[32,8,128]{2,1,0:T(8,128)S(1)} all-to-all(f32[32,8,128]{2,1,0:T(8,128)S(1)} %broadcast_in_dim.4), channel_id=1, replica_groups={{0,2,8,10,16,18,24,26,128,130,136,138,144,146,152,154,256,258,264,266,2..., dimensions={0} | all-to-all | bytes 262144 | tf_op jit(solution)/shard_map/all_to_all | solution.py:57
  36.6 1.0 %broadcast_in_dim.5 = f32[8,32,8,128]{3,2,1,0:T(8,128)} broadcast(f32[32,8,128]{2,1,0:T(8,128)S(1)} %all_to_all.20), dimensions={1,2,3} | broadcast | bytes 1179648 | tf_op jit(solution)/shard_map/broadcast_in_dim | solution.py:64
  37.6 3.6 %all-to-all-start.1 = ((f32[8,32,8,128]{3,2,1,0:T(8,128)}), f32[8,32,8,128]{3,2,1,0:T(8,128)S(1)}, u32[]{:S(2)}, u32[]{:S(2)}) async-start(f32[8,32,8,128]{3,2,1,0:T(8,128)} %broadcast_in_dim.5), calls=%async_computation.1 | async-start | bytes 2097152 | tf_op jit(solution)/shard_map/all_to_all | solution.py:57
  41.2 0.1 stack.26
  41.3 0.1 stack.24
  41.4 0.1 stack.25
  41.6 0.2 copy.8
  41.7 0.1 add_multiply_fusion.first_ref
  41.8 0.0 collective-permute-done.w1_ref
  41.8 4.7 %split.1 = (bf16[512,2048]{1,0:T(8,128)(2,1)}, bf16[512,2048]{1,0:T(8,128)(2,1)}) custom-call(f32[256,2048]{1,0:T(8,128)} %w0_ref.1, f32[256,2048]{1,0:T(8,128)} %collective-permute-done.w1_ref), custom_call_target="tpu_custom_call" | custom-call | flops 3145728 | bytes 8388608 | tf_op jit(solution)/shard_map/split/pallas_call | solution.py:101
  46.5 6.9 %all-to-all-done.1 = f32[8,32,8,128]{3,2,1,0:T(8,128)S(1)} async-done(((f32[8,32,8,128]{3,2,1,0:T(8,128)}), f32[8,32,8,128]{3,2,1,0:T(8,128)S(1)}, u32[]{:S(2)}, u32[]{:S(2)}) %all-to-all-start.1) | async-done | bytes 1048608 | tf_op jit(solution)/shard_map/all_to_all | solution.py:57
  53.4 5.4 %head.1 = (f32[128,256]{1,0:T(8,128)S(1)}, f32[128,256]{1,0:T(8,128)S(1)}, f32[4,2,4,8,8,128]{5,4,3,2,1,0:T(8,128)}) custom-call(s32[2]{0:T(128)S(1)} %add_multiply_fusion.first_ref, f32[128,3]{1,0:T(8,128)S(1)} %bitcast.13, f32[4,2,4,8,8,128]{5,4,3,2,1,0:T(8,128)S(1)} %bitcast.10, bf16[512,2048]{1,0:T(8,128)(2,1)} %get-tuple-element.7.high_ref, ...), custom_call_target="tpu_custom_call" | custom-call | flops 1610612736 | bytes 6291456 | tf_op jit(solution)/shard_map/head/pallas_call | solution.py:176
  58.8 3.6 %all-to-all-start.2 = ((f32[8,32,8,128]{3,2,1,0:T(8,128)}), f32[8,32,8,128]{3,2,1,0:T(8,128)S(1)}, u32[]{:S(2)}, u32[]{:S(2)}) async-start(f32[8,32,8,128]{3,2,1,0:T(8,128)} %bitcast.6), calls=%async_computation.2 | async-start | bytes 2097152 | tf_op jit(solution)/shard_map/all_to_all | solution.py:57
  62.4 1.9 %collective-permute-start.2 = (f32[4,2,4,8,8,128]{5,4,3,2,1,0:T(8,128)S(1)}, f32[4,2,4,8,8,128]{5,4,3,2,1,0:T(8,128)}, u32[]{:S(2)}, u32[]{:S(2)}) collective-permute-start(f32[4,2,4,8,8,128]{5,4,3,2,1,0:T(8,128)S(1)} %bitcast.11), channel_id=1, source_target_pairs={{0,1},{1,0},{2,3},{3,2},{4,5},{5,4},{6,7},{7,6},{8,9},{9,8},{10,11... | collective-permute-start | bytes 3145736 | tf_op jit(solution)/shard_map/ppermute | solution.py:53
  64.3 10.3 %all-to-all-done.2.x_ref = f32[8,32,8,128]{3,2,1,0:T(8,128)S(1)} async-done(((f32[8,32,8,128]{3,2,1,0:T(8,128)}), f32[8,32,8,128]{3,2,1,0:T(8,128)S(1)}, u32[]{:S(2)}, u32[]{:S(2)}) %all-to-all-start.2) | async-done | bytes 1048608 | tf_op jit(solution)/shard_map/all_to_all | solution.py:57
  74.6 0.7 local_sum.2
  75.2 7.0 %all-to-all-start.3 = ((f32[32,8,128]{2,1,0:T(8,128)}), f32[32,8,128]{2,1,0:T(8,128)S(1)}, u32[]{:S(2)}, u32[]{:S(2)}) async-start(f32[32,8,128]{2,1,0:T(8,128)} %local_sum.2), calls=%async_computation.3 | async-start | bytes 262144 | tf_op jit(solution)/shard_map/all_to_all | solution.py:57
  82.3 1.9 %collective-permute-start.1 = (f32[128,256]{1,0:T(8,128)S(1)}, f32[128,256]{1,0:T(8,128)S(1)}, u32[]{:S(2)}, u32[]{:S(2)}) collective-permute-start(f32[128,256]{1,0:T(8,128)S(1)} %get-tuple-element.11), channel_id=1, source_target_pairs={{0,1},{1,0},{2,3},{3,2},{4,5},{5,4},{6,7},{7,6},{8,9},{9,8},{10,11... | collective-permute-start | bytes 393224 | tf_op jit(solution)/shard_map/ppermute | solution.py:53
  84.2 1.3 %collective-permute-done.1.d1_ref = f32[128,256]{1,0:T(8,128)S(1)} collective-permute-done((f32[128,256]{1,0:T(8,128)S(1)}, f32[128,256]{1,0:T(8,128)S(1)}, u32[]{:S(2)}, u32[]{:S(2)}) %collective-permute-start.1) | collective-permute-done | bytes 131104 | tf_op jit(solution)/shard_map/ppermute | solution.py:53
  85.5 3.6 %weight_grad.1 = f32[256,2048]{1,0:T(8,128)} custom-call(f32[128,256]{1,0:T(8,128)S(1)} %get-tuple-element.10.d0_ref, f32[128,256]{1,0:T(8,128)S(1)} %collective-permute-done.1.d1_ref, f32[4,2,4,8,8,128]{5,4,3,2,1,0:T(8,128)S(1)} %bitcast.12, f32[4,2,4,8,8,128]{5,4,3,2,1,0:T(8,128)} %collective-permute-done.2.x1_ref), custom_call_target="tpu_custom_call" | custom-call | flops 805306368 | bytes 5242880 | tf_op jit(solution)/shard_map/weight_grad/pallas_call | solution.py:209
  89.1 6.6 %all-to-all-done.3.x_ref = f32[32,8,128]{2,1,0:T(8,128)S(1)} async-done(((f32[32,8,128]{2,1,0:T(8,128)}), f32[32,8,128]{2,1,0:T(8,128)S(1)}, u32[]{:S(2)}, u32[]{:S(2)}) %all-to-all-start.3) | async-done | bytes 131104 | tf_op jit(solution)/shard_map/all_to_all | solution.py:57
  95.8 0.6 local_sum.3
  (10 shorter events, 0.1 us)
Async XLA Ops:
  0.6 40.5 %copy-start.2 = (s32[256]{0:T(256)S(1)}, s32[256]{0:T(256)}, u32[]{:S(2)}) copy-start(s32[256]{0:T(256)} %param.8) | copy-start | bytes 3076
  0.6 40.7 %copy-start = (f32[256]{0:T(256)S(1)}, f32[256]{0:T(256)}, u32[]{:S(2)}) copy-start(f32[256]{0:T(256)} %param.7) | copy-start | bytes 3076
  0.7 40.8 %copy-start.1 = (f32[256]{0:T(256)S(1)}, f32[256]{0:T(256)}, u32[]{:S(2)}) copy-start(f32[256]{0:T(256)} %param.9) | copy-start | bytes 3076
  0.7 41.2 %collective-permute-start = (f32[256,2048]{1,0:T(8,128)}, f32[256,2048]{1,0:T(8,128)}, u32[]{:S(2)}, u32[]{:S(2)}) collective-permute-start(f32[256,2048]{1,0:T(8,128)} %w0_ref.1), channel_id=1, source_target_pairs={{0,1},{1,0},{2,3},{3,2},{4,5},{5,4},{6,7},{7,6},{8,9},{9,8},{10,11... | collective-permute-start | bytes 6291464 | tf_op jit(solution)/shard_map/ppermute | solution.py:53
  37.6 15.8 %all-to-all-start.1 = ((f32[8,32,8,128]{3,2,1,0:T(8,128)}), f32[8,32,8,128]{3,2,1,0:T(8,128)S(1)}, u32[]{:S(2)}, u32[]{:S(2)}) async-start(f32[8,32,8,128]{3,2,1,0:T(8,128)} %broadcast_in_dim.5), calls=%async_computation.1 | async-start | bytes 2097152 | tf_op jit(solution)/shard_map/all_to_all | solution.py:57
  58.8 15.8 %all-to-all-start.2 = ((f32[8,32,8,128]{3,2,1,0:T(8,128)}), f32[8,32,8,128]{3,2,1,0:T(8,128)S(1)}, u32[]{:S(2)}, u32[]{:S(2)}) async-start(f32[8,32,8,128]{3,2,1,0:T(8,128)} %bitcast.6), calls=%async_computation.2 | async-start | bytes 2097152 | tf_op jit(solution)/shard_map/all_to_all | solution.py:57
  62.4 23.2 %collective-permute-start.2 = (f32[4,2,4,8,8,128]{5,4,3,2,1,0:T(8,128)S(1)}, f32[4,2,4,8,8,128]{5,4,3,2,1,0:T(8,128)}, u32[]{:S(2)}, u32[]{:S(2)}) collective-permute-start(f32[4,2,4,8,8,128]{5,4,3,2,1,0:T(8,128)S(1)} %bitcast.11), channel_id=1, source_target_pairs={{0,1},{1,0},{2,3},{3,2},{4,5},{5,4},{6,7},{7,6},{8,9},{9,8},{10,11... | collective-permute-start | bytes 3145736 | tf_op jit(solution)/shard_map/ppermute | solution.py:53
  75.2 20.5 %all-to-all-start.3 = ((f32[32,8,128]{2,1,0:T(8,128)}), f32[32,8,128]{2,1,0:T(8,128)S(1)}, u32[]{:S(2)}, u32[]{:S(2)}) async-start(f32[32,8,128]{2,1,0:T(8,128)} %local_sum.2), calls=%async_computation.3 | async-start | bytes 262144 | tf_op jit(solution)/shard_map/all_to_all | solution.py:57
  82.3 3.2 %collective-permute-start.1 = (f32[128,256]{1,0:T(8,128)S(1)}, f32[128,256]{1,0:T(8,128)S(1)}, u32[]{:S(2)}, u32[]{:S(2)}) collective-permute-start(f32[128,256]{1,0:T(8,128)S(1)} %get-tuple-element.11), channel_id=1, source_target_pairs={{0,1},{1,0},{2,3},{3,2},{4,5},{5,4},{6,7},{7,6},{8,9},{9,8},{10,11... | collective-permute-start | bytes 393224 | tf_op jit(solution)/shard_map/ppermute | solution.py:53

commit v3 on v2

--- a/solution.py
+++ b/solution.py
@@ -43,8 +43,8 @@
 ROWS = 256
 D = 2048
 CHUNK = 512
-SPLIT_VMEM, HEAD_VMEM = 62, 50
-PIECES = 4
+HEAD_VMEM = 50
+PIECES = 2
 NCH = D // CHUNK
 TILES = (4, 2, 4, 8, 8, 128)
 
@@ -89,37 +89,16 @@
     return high, jnp.concatenate([high, low], axis=0)
 
 
-def split_kernel(w0_ref, w1_ref, high_ref, low_ref):
-    for k, w in ((0, w0_ref), (1, w1_ref)):
-        rows = pl.ds(k * ROWS, ROWS)
-        high_ref[rows], low_ref[rows] = parts(w[...])
-
-
-def split(w0, w1):
-    vmem = pl.BlockSpec(memory_space=pltpu.VMEM)
-    out = jax.ShapeDtypeStruct((2 * ROWS, D), jnp.bfloat16)
-    return pl.pallas_call(
-        split_kernel,
-        out_shape=(out, out),
-        in_specs=[vmem, vmem],
-        out_specs=(vmem, vmem),
-        compiler_params=pltpu.CompilerParams(vmem_limit_bytes=SPLIT_VMEM << 20),
-        cost_estimate=pl.CostEstimate(
-            flops=6 * ROWS * D, bytes_accessed=8 << 20, transcendentals=0
-        ),
-        name="split",
-    )(w0, w1)
-
-
 def head_kernel(
     first_ref,
     vec_ref,
     x_ref,
-    high_ref,
-    low_ref,
+    w0_ref,
+    w1_ref,
     dl0_ref,
     dl1_ref,
     part_ref,
+    w,
     high,
     low,
     xs,
@@ -128,22 +107,26 @@
     outs,
 ):
     fetches = []
-    for p, (src, dst) in enumerate(((high_ref, high), (low_ref, low))):
+    n = ROWS // PIECES
+    for k, src in enumerate((w0_ref, w1_ref)):
         for i in range(PIECES):
-            rows = pl.ds(i * (2 * ROWS // PIECES), 2 * ROWS // PIECES)
             fetches.append(
-                pltpu.make_async_copy(src.at[rows], dst.at[rows], ins.at[p, i])
+                pltpu.make_async_copy(
+                    src.at[pl.ds(i * n, n)],
+                    w.at[pl.ds(k * ROWS + i * n, n)],
+                    ins.at[k, i],
+                )
             )
             fetches[-1].start()
     for j in range(NCH):
         for f in range(4):
             cols = pl.ds(j * CHUNK + f * 128, 128)
             xs[:TOK, cols], xs[TOK:, cols] = parts(x_ref[f, :, j].reshape(TOK, 128))
-    for fetch in fetches[:PIECES]:
+    for i, fetch in enumerate(fetches):
         fetch.wait()
+        rows = pl.ds(i * n, n)
+        high[rows], low[rows] = parts(w[rows])
     both = dot(xs[...], high[...], ((1,), (1,)))
-    for fetch in fetches[PIECES:]:
-        fetch.wait()
     logits = both[:TOK] + both[TOK:] + dot(xs[:TOK], low[...], ((1,), (1,)))
     log_norm, grad, target = vec_ref[:, 0:1], vec_ref[:, 1:2], vec_ref[:, 2:3]
     target = target.astype(jnp.int32)
@@ -169,7 +152,7 @@
         copy.wait()
 
 
-def head(first, vec, x, high, low):
+def head(first, vec, x, w0, w1):
     vmem = pl.BlockSpec(memory_space=pltpu.VMEM)
     hbm = pl.BlockSpec(memory_space=pl.ANY)
     dl = jax.ShapeDtypeStruct((TOK, ROWS), jnp.float32)
@@ -179,6 +162,7 @@
         in_specs=[pl.BlockSpec(memory_space=pltpu.SMEM), vmem, vmem, hbm, hbm],
         out_specs=(vmem, vmem, hbm),
         scratch_shapes=[
+            pltpu.VMEM((2 * ROWS, D), jnp.float32),
             pltpu.VMEM((2 * ROWS, D), jnp.bfloat16),
             pltpu.VMEM((2 * ROWS, D), jnp.bfloat16),
             pltpu.VMEM((2 * TOK, D), jnp.bfloat16),
@@ -193,7 +177,7 @@
             transcendentals=2 * TOK * ROWS,
         ),
         name="head",
-    )(first, vec, x, high, low)
+    )(first, vec, x, w0, w1)
 
 
 def weight_grad_kernel(d0_ref, d1_ref, x0_ref, x1_ref, out_ref):
@@ -249,10 +233,10 @@
     first = jnp.stack([shard, shard + 1 - 2 * c]).astype(jnp.int32) * ROWS
 
     far = spread(hidden, FAR)
-    other_weight = swap(weight)
+    own_weight, far = lax.optimization_barrier((weight, far))
+    other_weight = swap(own_weight)
     near = spread(far, NEAR).reshape(TILES)
-    high, low = split(weight, other_weight)
-    dl0, dl1, part = head(first, vec, near, high, low)
+    dl0, dl1, part = head(first, vec, near, own_weight, other_weight)
     got = part.reshape(8, 32, 8, 128)
     got = exchange(got, NEAR)
     got = local_sum(got)

time: 96.9 us -> 99.2 us (1.024)
  blocking collectives: 26.3 us -> 32.4 us
  waiting for transfers between devices: 25.1 us -> 31 us
  starting transfers between devices: 26.9 us -> 21.4 us
  Pallas kernels: 15 us -> 9.6 us
  local copies, waits for them, and re-layouts: 2.2 us -> 3.54 us
    all_to_all x1, blocking collectives: 26.3 us -> 32.4 us  [exchange(): lax.all_to_all(x, PIPE + DP, 0, 0, axis_index_groups=groups, tiled=True)]
    all_to_all x3, waiting for transfers between devices: 23.8 us -> 29.7 us  [exchange(): lax.all_to_all(x, PIPE + DP, 0, 0, axis_index_groups=groups, tiled=True)]
    ppermute x3, starting transfers between devices: 12.7 us -> 7.75 us  [swap(): return lax.ppermute(x, 'c', [(0, 1), (1, 0)])]
    pallas_call x1 -> x0, Pallas kernels: 4.66 us -> none  [split(): pl.pallas_call(split_kernel, out_shape=(out, out), in_specs=[vmem, vmem],...]
    unnamed x6 -> x8, local copies, waits for them, and re-layouts: 0.01 us -> 1.33 us
    pallas_call x1, Pallas kernels: 3.58 us -> 2.36 us  [weight_grad(): pl.pallas_call(weight_grad_kernel, out_shape=jax.ShapeDtypeStruct((ROWS,...]
  transfers between devices with their start and end apart: 6 -> 6, of which waited for: 4 -> 4; matrix products, arithmetic and copies ran while one was open for 2% -> 2% of each run, Pallas kernels for 9% -> 3%
where the time goes in v3:
time: 99.2 us; the launch traced here: 98.8 us
  blocking collectives  32.4 us (33%)
  waiting for transfers between devices  31 us (31%)
  starting transfers between devices  21.4 us (22%)
  Pallas kernels  9.6 us (10%)
  local copies, waits for them, and re-layouts  3.54 us (4%)
    all_to_all x1, blocking collectives, exchange(): lax.all_to_all(x, PIPE + DP, 0, 0, axis_index_groups=groups, tiled=True)  32.4 us
    all_to_all x3, waiting for transfers between devices, exchange(): lax.all_to_all(x, PIPE + DP, 0, 0, axis_index_groups=groups, tiled=True)  29.7 us
    all_to_all x3, starting transfers between devices, exchange(): lax.all_to_all(x, PIPE + DP, 0, 0, axis_index_groups=groups, tiled=True)  13.6 us
    ppermute x3, starting transfers between devices, swap(): return lax.ppermute(x, 'c', [(0, 1), (1, 0)])  7.75 us
    pallas_call x1, Pallas kernels, head(): pl.pallas_call(head_kernel, out_shape=(dl, dl, jax.ShapeDtypeStruct(TILES...  5.91 us
    pallas_call x1, Pallas kernels, weight_grad(): pl.pallas_call(weight_grad_kernel, out_shape=jax.ShapeDtypeStruct((ROWS,...  2.36 us
  transfers between devices with their start and end apart: 6, of which 4 were waited for; matrix products, arithmetic and copies ran while one was open for 2% of the time, Pallas kernels for 3%

profile of v3, /device:TPU:1, one launch (start us, length us, event | category | flops | bytes accessed | tf_op | source)
XLA Modules:
  0.0 98.8 jit_solution(7019692060711780497)
XLA Ops:
  0.7 0.7 broadcast_in_dim.4
  1.4 32.4 %all_to_all.20 = f32[32,8,128]{2,1,0:T(8,128)S(1)} all-to-all(f32[32,8,128]{2,1,0:T(8,128)S(1)} %broadcast_in_dim.4), channel_id=1, replica_groups={{0,2,8,10,16,18,24,26,128,130,136,138,144,146,152,154,256,258,264,266,2..., dimensions={0} | all-to-all | bytes 262144 | tf_op jit(solution)/shard_map/all_to_all | solution.py:57
  33.7 3.9 %collective-permute-start = (f32[256,2048]{1,0:T(8,128)}, f32[256,2048]{1,0:T(8,128)S(1)}, u32[]{:S(2)}, u32[]{:S(2)}) collective-permute-start(f32[256,2048]{1,0:T(8,128)} %w0_ref), channel_id=1, source_target_pairs={{0,1},{1,0},{2,3},{3,2},{4,5},{5,4},{6,7},{7,6},{8,9},{9,8},{10,11... | collective-permute-start | bytes 6291464 | tf_op jit(solution)/shard_map/ppermute | solution.py:53
  37.7 1.0 %broadcast_in_dim.5 = f32[8,32,8,128]{3,2,1,0:T(8,128)} broadcast(f32[32,8,128]{2,1,0:T(8,128)S(1)} %all_to_all.20), dimensions={1,2,3} | broadcast | bytes 1179648 | tf_op jit(solution)/shard_map/broadcast_in_dim | solution.py:64
  38.7 3.6 %all-to-all-start.1 = ((f32[8,32,8,128]{3,2,1,0:T(8,128)}), f32[8,32,8,128]{3,2,1,0:T(8,128)S(1)}, u32[]{:S(2)}, u32[]{:S(2)}) async-start(f32[8,32,8,128]{3,2,1,0:T(8,128)} %broadcast_in_dim.5), calls=%async_computation.1 | async-start | bytes 2097152 | tf_op jit(solution)/shard_map/all_to_all | solution.py:57
  42.3 0.1 stack.24
  42.4 0.1 stack.25
  42.5 0.1 stack.26
  42.7 0.2 copy.8
  42.8 0.1 add_multiply_fusion.first_ref
  42.9 11.5 %all-to-all-done.1 = f32[8,32,8,128]{3,2,1,0:T(8,128)S(1)} async-done(((f32[8,32,8,128]{3,2,1,0:T(8,128)}), f32[8,32,8,128]{3,2,1,0:T(8,128)S(1)}, u32[]{:S(2)}, u32[]{:S(2)}) %all-to-all-start.1) | async-done | bytes 1048608 | tf_op jit(solution)/shard_map/all_to_all | solution.py:57
  54.5 0.0 collective-permute-done.w1_ref
  54.5 1.3 %copy-done.3 = f32[256,2048]{1,0:T(8,128)} copy-done((f32[256,2048]{1,0:T(8,128)}, f32[256,2048]{1,0:T(8,128)S(1)}, u32[]{:S(2)}) %copy-start.3) | copy-done | bytes 2097176
  55.8 5.9 %head.1 = (f32[128,256]{1,0:T(8,128)S(1)}, f32[128,256]{1,0:T(8,128)S(1)}, f32[4,2,4,8,8,128]{5,4,3,2,1,0:T(8,128)}) custom-call(s32[2]{0:T(128)S(1)} %add_multiply_fusion.first_ref, f32[128,3]{1,0:T(8,128)S(1)} %bitcast.13, f32[4,2,4,8,8,128]{5,4,3,2,1,0:T(8,128)S(1)} %bitcast.10, f32[256,2048]{1,0:T(8,128)} %w0_ref, f32[256,2048]{1,0:T(8,128)} %copy-done.3), custom_call_target="tpu_custom_call" | custom-call | flops 1610612736 | bytes 6291456 | tf_op jit(solution)/shard_map/head/pallas_call | solution.py:159
  61.7 3.6 %all-to-all-start.2 = ((f32[8,32,8,128]{3,2,1,0:T(8,128)}), f32[8,32,8,128]{3,2,1,0:T(8,128)S(1)}, u32[]{:S(2)}, u32[]{:S(2)}) async-start(f32[8,32,8,128]{3,2,1,0:T(8,128)} %bitcast.6), calls=%async_computation.2 | async-start | bytes 2097152 | tf_op jit(solution)/shard_map/all_to_all | solution.py:57
  65.3 1.9 %collective-permute-start.2 = (f32[4,2,4,8,8,128]{5,4,3,2,1,0:T(8,128)S(1)}, f32[4,2,4,8,8,128]{5,4,3,2,1,0:T(8,128)S(1)}, u32[]{:S(2)}, u32[]{:S(2)}) collective-permute-start(f32[4,2,4,8,8,128]{5,4,3,2,1,0:T(8,128)S(1)} %bitcast.11), channel_id=1, source_target_pairs={{0,1},{1,0},{2,3},{3,2},{4,5},{5,4},{6,7},{7,6},{8,9},{9,8},{10,11... | collective-permute-start | bytes 3145736 | tf_op jit(solution)/shard_map/ppermute | solution.py:53
  67.2 10.3 %all-to-all-done.2.x_ref = f32[8,32,8,128]{3,2,1,0:T(8,128)S(1)} async-done(((f32[8,32,8,128]{3,2,1,0:T(8,128)}), f32[8,32,8,128]{3,2,1,0:T(8,128)S(1)}, u32[]{:S(2)}, u32[]{:S(2)}) %all-to-all-start.2) | async-done | bytes 1048608 | tf_op jit(solution)/shard_map/all_to_all | solution.py:57
  77.5 0.7 local_sum.2
  78.2 6.5 %all-to-all-start.3 = ((f32[32,8,128]{2,1,0:T(8,128)}), f32[32,8,128]{2,1,0:T(8,128)S(1)}, u32[]{:S(2)}, u32[]{:S(2)}) async-start(f32[32,8,128]{2,1,0:T(8,128)} %local_sum.2), calls=%async_computation.3 | async-start | bytes 262144 | tf_op jit(solution)/shard_map/all_to_all | solution.py:57
  84.7 1.9 %collective-permute-start.1 = (f32[128,256]{1,0:T(8,128)S(1)}, f32[128,256]{1,0:T(8,128)S(1)}, u32[]{:S(2)}, u32[]{:S(2)}) collective-permute-start(f32[128,256]{1,0:T(8,128)S(1)} %get-tuple-element.11), channel_id=1, source_target_pairs={{0,1},{1,0},{2,3},{3,2},{4,5},{5,4},{6,7},{7,6},{8,9},{9,8},{10,11... | collective-permute-start | bytes 393224 | tf_op jit(solution)/shard_map/ppermute | solution.py:53
  86.6 1.3 %collective-permute-done.1.d1_ref = f32[128,256]{1,0:T(8,128)S(1)} collective-permute-done((f32[128,256]{1,0:T(8,128)S(1)}, f32[128,256]{1,0:T(8,128)S(1)}, u32[]{:S(2)}, u32[]{:S(2)}) %collective-permute-start.1) | collective-permute-done | bytes 131104 | tf_op jit(solution)/shard_map/ppermute | solution.py:53
  87.9 2.4 %weight_grad.1 = f32[256,2048]{1,0:T(8,128)} custom-call(f32[128,256]{1,0:T(8,128)S(1)} %get-tuple-element.10.d0_ref, f32[128,256]{1,0:T(8,128)S(1)} %collective-permute-done.1.d1_ref, f32[4,2,4,8,8,128]{5,4,3,2,1,0:T(8,128)S(1)} %bitcast.12, f32[4,2,4,8,8,128]{5,4,3,2,1,0:T(8,128)S(1)} %collective-permute-done.2.x1_ref), custom_call_target="tpu_custom_call" | custom-call | flops 805306368 | bytes 5242880 | tf_op jit(solution)/shard_map/weight_grad/pallas_call | solution.py:193
  90.3 7.9 %all-to-all-done.3.x_ref = f32[32,8,128]{2,1,0:T(8,128)S(1)} async-done(((f32[32,8,128]{2,1,0:T(8,128)}), f32[32,8,128]{2,1,0:T(8,128)S(1)}, u32[]{:S(2)}, u32[]{:S(2)}) %all-to-all-start.3) | async-done | bytes 131104 | tf_op jit(solution)/shard_map/all_to_all | solution.py:57
  98.1 0.6 local_sum.3
  (11 shorter events, 0.1 us)
Async XLA Ops:
  0.6 41.6 %copy-start = (f32[256]{0:T(256)S(1)}, f32[256]{0:T(256)}, u32[]{:S(2)}) copy-start(f32[256]{0:T(256)} %param.7) | copy-start | bytes 3076
  0.6 41.7 %copy-start.1 = (f32[256]{0:T(256)S(1)}, f32[256]{0:T(256)}, u32[]{:S(2)}) copy-start(f32[256]{0:T(256)} %param.9) | copy-start | bytes 3076
  0.7 41.8 %copy-start.2 = (s32[256]{0:T(256)S(1)}, s32[256]{0:T(256)}, u32[]{:S(2)}) copy-start(s32[256]{0:T(256)} %param.8) | copy-start | bytes 3076
  33.7 20.7 %collective-permute-start = (f32[256,2048]{1,0:T(8,128)}, f32[256,2048]{1,0:T(8,128)S(1)}, u32[]{:S(2)}, u32[]{:S(2)}) collective-permute-start(f32[256,2048]{1,0:T(8,128)} %w0_ref), channel_id=1, source_target_pairs={{0,1},{1,0},{2,3},{3,2},{4,5},{5,4},{6,7},{7,6},{8,9},{9,8},{10,11... | collective-permute-start | bytes 6291464 | tf_op jit(solution)/shard_map/ppermute | solution.py:53
  38.7 15.8 %all-to-all-start.1 = ((f32[8,32,8,128]{3,2,1,0:T(8,128)}), f32[8,32,8,128]{3,2,1,0:T(8,128)S(1)}, u32[]{:S(2)}, u32[]{:S(2)}) async-start(f32[8,32,8,128]{3,2,1,0:T(8,128)} %broadcast_in_dim.5), calls=%async_computation.1 | async-start | bytes 2097152 | tf_op jit(solution)/shard_map/all_to_all | solution.py:57
  54.5 1.3 %copy-start.3 = (f32[256,2048]{1,0:T(8,128)}, f32[256,2048]{1,0:T(8,128)S(1)}, u32[]{:S(2)}) copy-start(f32[256,2048]{1,0:T(8,128)S(1)} %collective-permute-done.w1_ref) | copy-start | bytes 6291460
  61.7 15.8 %all-to-all-start.2 = ((f32[8,32,8,128]{3,2,1,0:T(8,128)}), f32[8,32,8,128]{3,2,1,0:T(8,128)S(1)}, u32[]{:S(2)}, u32[]{:S(2)}) async-start(f32[8,32,8,128]{3,2,1,0:T(8,128)} %bitcast.6), calls=%async_computation.2 | async-start | bytes 2097152 | tf_op jit(solution)/shard_map/all_to_all | solution.py:57
  65.3 22.6 %collective-permute-start.2 = (f32[4,2,4,8,8,128]{5,4,3,2,1,0:T(8,128)S(1)}, f32[4,2,4,8,8,128]{5,4,3,2,1,0:T(8,128)S(1)}, u32[]{:S(2)}, u32[]{:S(2)}) collective-permute-start(f32[4,2,4,8,8,128]{5,4,3,2,1,0:T(8,128)S(1)} %bitcast.11), channel_id=1, source_target_pairs={{0,1},{1,0},{2,3},{3,2},{4,5},{5,4},{6,7},{7,6},{8,9},{9,8},{10,11... | collective-permute-start | bytes 3145736 | tf_op jit(solution)/shard_map/ppermute | solution.py:53
  78.2 20.0 %all-to-all-start.3 = ((f32[32,8,128]{2,1,0:T(8,128)}), f32[32,8,128]{2,1,0:T(8,128)S(1)}, u32[]{:S(2)}, u32[]{:S(2)}) async-start(f32[32,8,128]{2,1,0:T(8,128)} %local_sum.2), calls=%async_computation.3 | async-start | bytes 262144 | tf_op jit(solution)/shard_map/all_to_all | solution.py:57
  84.7 3.2 %collective-permute-start.1 = (f32[128,256]{1,0:T(8,128)S(1)}, f32[128,256]{1,0:T(8,128)S(1)}, u32[]{:S(2)}, u32[]{:S(2)}) collective-permute-start(f32[128,256]{1,0:T(8,128)S(1)} %get-tuple-element.11), channel_id=1, source_target_pairs={{0,1},{1,0},{2,3},{3,2},{4,5},{5,4},{6,7},{7,6},{8,9},{9,8},{10,11... | collective-permute-start | bytes 393224 | tf_op jit(solution)/shard_map/ppermute | solution.py:53
